TPU v7x, 256 devices: a whole 4x4x8 slice. The times are simulated.
256 devices in a mesh: blk: 8 (over x_hi, y), group: 32 (over z, x_lo, core).
Axes of the slice: x: 4 (x_hi: 2, x_lo: 2; x = x_hi * 2 + x_lo), y: 4, z: 8, core: 2. Of those that a mesh axis runs over, the one named last changes fastest.
Arguments:
- walk_rows: bfloat16 [4096, 131072], P('blk', 'group'), may hold values from -6 to 6
- col_values: bfloat16 [49152, 4096], P('group', 'blk'), may hold values from -0.02734375 to 0.02734375
- col_index: int32 [96, 8], P('group'), may hold values from 0 to 7
- col_count: int32 [32, 8], P('group'), may hold values from 1 to 3, as said below
Outputs:
- inflated: float32 [4096, 4096], P(('blk', 'group'))
Inputs may be any that keep to these rules, and one draw needn't show every extreme that they name: `col_count`: each list holds 1 to 3 valid slots; some list holds 3; contents of the other slots are arbitrary.
All inputs are finite; a program needn't handle non-finite values.
Results may differ from a plain program's by a relative error of at most 0.0003.
Values may be sent and summed in bfloat16 or wider, within the bound.
No kernel may reach another device: no remote copies, remote signals or barrier semaphores. Data moves between devices by JAX's collectives and lax.ppermute only.
A program may use at most 64 MiB of HBM per device.

v0:
```python
import jax
import jax.numpy as jnp
from jax import lax
from jax.sharding import PartitionSpec as P


def shifted(shard, axis, by):
    size = lax.axis_size(axis)
    return lax.ppermute(shard, axis, [(i, (i + by) % size) for i in range(size)])


def on_device(walk_rows, col_values, col_index, col_count):
    width = col_values.shape[1]
    slots = col_values.shape[0] // width
    nblock = lax.axis_size("blk")
    myself = lax.axis_index("blk")
    rows_here = walk_rows.shape[0]
    share = rows_here // lax.axis_size("group")

    def panel_product(rows, values, panel):
        index = lax.dynamic_slice_in_dim(col_index, panel, 1, 1)[:, 0]
        count = lax.dynamic_slice_in_dim(col_count, panel, 1, 1)[0, 0]
        total = jnp.zeros((rows.shape[0], width), jnp.float32)
        for slot in range(slots):
            block = lax.dynamic_slice_in_dim(rows, index[slot] * width, width, 1)
            piece = values[slot * width : (slot + 1) * width]
            product = jnp.dot(block, piece, preferred_element_type=jnp.float32)
            total = total + jnp.where(slot < count, product, jnp.zeros_like(product))
        return total

    def turn(step, carry):
        values, result = carry
        panel = (myself - step) % nblock
        part = panel_product(walk_rows, values, panel)
        reduced = lax.psum_scatter(part, "group", scatter_dimension=0, tiled=True)
        result = lax.dynamic_update_slice_in_dim(result, reduced, panel * width, 1)
        values = shifted(values, "blk", 1)
        return (values, result)

    start_out = jnp.zeros((share, nblock * width), jnp.float32)
    unused, expanded = lax.fori_loop(0, nblock, turn, (col_values, start_out))
    squared = expanded * expanded
    column = jnp.sum(squared, axis=0)
    total = lax.psum(column, ("blk", "group"))
    scale = total / (nblock * rows_here) + 1e-06
    return squared / scale


def solution(mesh):
    return jax.shard_map(
        on_device,
        mesh=mesh,
        in_specs=(P("blk", "group"), P("group", "blk"), P("group", None), P("group", None)),
        out_specs=P(("blk", "group"), None),
        check_vma=False,
    )
```

profile of v0, /device:TPU:1, one launch (start us, length us, event | category | flops | bytes accessed | tf_op | source)
XLA Modules:
  0.0 1125.3 jit_solution(7067308069750690020)
XLA Ops:
  7.9 1030.1 %while.17 = (s32[]{:T(128)}, bf16[1536,512]{1,0:T(8,128)(2,1)S(1)}, f32[16,4096]{1,0:T(8,128)S(1)}, s32[]{:T(128)}, s32[1,8]{1,0:T(1,128)S(1)}, /*index=5*/s32[3...) while((s32[]{:T(128)}, bf16[1536,512]{1,0:T(8,128)(2,1)S(1)}, ...), condition=%wide.region_2.3_spmd, body=%wide.region_0.2_spmd.sunk | while | flops 806617088 | bytes 21137560 | solution.py:41
  12.4 2.1 convolution_select_fusion.5
  16.0 2.5 fusion.30
  18.5 2.2 collective-permute-start
  20.7 117.8 %reduce-scatter.2.cloned.1.call-done = f32[16,512]{1,0:T(8,128)} async-done(((f32[512,512]{1,0:T(8,128)}), f32[16,512]{1,0:T(8,128)}) %reduce-scatter.2.cloned.1.call-update) | async-done | bytes 32784 | tf_op jit(solution)/shard_map/while/body/eval_jaxpr/reduce_scatter | solution.py:35
  143.7 2.1 convolution_select_fusion.5
  147.3 2.5 fusion.30
  149.9 117.1 %reduce-scatter.2.cloned.1.call-done = f32[16,512]{1,0:T(8,128)} async-done(((f32[512,512]{1,0:T(8,128)}), f32[16,512]{1,0:T(8,128)}) %reduce-scatter.2.cloned.1.call-update) | async-done | bytes 32784 | tf_op jit(solution)/shard_map/while/body/eval_jaxpr/reduce_scatter | solution.py:35
  272.2 2.1 convolution_select_fusion.5
  274.3 1.5 convolution_select_fusion.6
  275.8 2.5 fusion.30
  278.4 116.7 %reduce-scatter.2.cloned.1.call-done = f32[16,512]{1,0:T(8,128)} async-done(((f32[512,512]{1,0:T(8,128)}), f32[16,512]{1,0:T(8,128)}) %reduce-scatter.2.cloned.1.call-update) | async-done | bytes 32784 | tf_op jit(solution)/shard_map/while/body/eval_jaxpr/reduce_scatter | solution.py:35
  400.4 2.1 convolution_select_fusion.5
  402.5 1.5 convolution_select_fusion.6
  404.0 2.5 fusion.30
  406.6 116.8 %reduce-scatter.2.cloned.1.call-done = f32[16,512]{1,0:T(8,128)} async-done(((f32[512,512]{1,0:T(8,128)}), f32[16,512]{1,0:T(8,128)}) %reduce-scatter.2.cloned.1.call-update) | async-done | bytes 32784 | tf_op jit(solution)/shard_map/while/body/eval_jaxpr/reduce_scatter | solution.py:35
  528.7 2.1 convolution_select_fusion.5
  532.3 2.5 fusion.30
  535.0 116.8 %reduce-scatter.2.cloned.1.call-done = f32[16,512]{1,0:T(8,128)} async-done(((f32[512,512]{1,0:T(8,128)}), f32[16,512]{1,0:T(8,128)}) %reduce-scatter.2.cloned.1.call-update) | async-done | bytes 32784 | tf_op jit(solution)/shard_map/while/body/eval_jaxpr/reduce_scatter | solution.py:35
  657.1 2.1 convolution_select_fusion.5
  659.2 1.5 convolution_select_fusion.6
  660.7 2.5 fusion.30
  663.5 116.9 %reduce-scatter.2.cloned.1.call-done = f32[16,512]{1,0:T(8,128)} async-done(((f32[512,512]{1,0:T(8,128)}), f32[16,512]{1,0:T(8,128)}) %reduce-scatter.2.cloned.1.call-update) | async-done | bytes 32784 | tf_op jit(solution)/shard_map/while/body/eval_jaxpr/reduce_scatter | solution.py:35
  785.6 2.1 convolution_select_fusion.5
  787.7 1.5 convolution_select_fusion.6
  789.2 2.5 fusion.30
  791.9 116.9 %reduce-scatter.2.cloned.1.call-done = f32[16,512]{1,0:T(8,128)} async-done(((f32[512,512]{1,0:T(8,128)}), f32[16,512]{1,0:T(8,128)}) %reduce-scatter.2.cloned.1.call-update) | async-done | bytes 32784 | tf_op jit(solution)/shard_map/while/body/eval_jaxpr/reduce_scatter | solution.py:35
  914.0 2.1 convolution_select_fusion.5
  916.1 1.5 convolution_select_fusion.6
  917.6 2.5 fusion.30
  920.6 116.6 %reduce-scatter.2.cloned.1.call-done = f32[16,512]{1,0:T(8,128)} async-done(((f32[512,512]{1,0:T(8,128)}), f32[16,512]{1,0:T(8,128)}) %reduce-scatter.2.cloned.1.call-update) | async-done | bytes 32784 | tf_op jit(solution)/shard_map/while/body/eval_jaxpr/reduce_scatter | solution.py:35
  1038.1 79.7 %psum.7 = f32[4096]{0:T(1024)S(1)} all-reduce(f32[4096]{0:T(1024)S(1)} %multiply_reduce_fusion), channel_id=1, replica_groups=mesh['blk'=8,'group'=32] {'blk','group'}, use_global_device_ids=true, to_apply=%region_4.5 | all-reduce | flops 4096 | bytes 32768 | tf_op jit(solution)/shard_map/psum | solution.py:44
  (84 shorter events, 25.8 us)
Async XLA Ops:
  6.5 1.4 copy-start
  6.5 1.4 copy-start.1
  6.5 1.4 copy-start.2
  7.9 130.5 %reduce-scatter.2.cloned.1.call-start = ((), (), s32[]{:S(2)}) async-start(), calls=%async_computation.1 | async-start | bytes 1081344 | tf_op jit(solution)/shard_map/while/body/eval_jaxpr/reduce_scatter | solution.py:35
  18.5 120.8 %collective-permute-start = (bf16[1536,512]{1,0:T(8,128)(2,1)S(1)}, bf16[1536,512]{1,0:T(8,128)(2,1)S(1)}, u32[]{:S(2)}, u32[]{:S(2)}) collective-permute-start(bf16[1536,512]{1,0:T(8,128)(2,1)S(1)} %copy.10), channel_id=1, source_target_pairs={{0,32},{32,64},{64,96},{96,128},{128,160},{160,192},{192,224},{224... | collective-permute-start | bytes 4718600 | tf_op jit(solution)/shard_map/while/body/eval_jaxpr/ppermute | solution.py:9
  139.3 127.7 %reduce-scatter.2.cloned.1.call-start = ((), (), s32[]{:S(2)}) async-start(), calls=%async_computation.1 | async-start | bytes 1081344 | tf_op jit(solution)/shard_map/while/body/eval_jaxpr/reduce_scatter | solution.py:35
  149.8 117.9 %collective-permute-start = (bf16[1536,512]{1,0:T(8,128)(2,1)S(1)}, bf16[1536,512]{1,0:T(8,128)(2,1)S(1)}, u32[]{:S(2)}, u32[]{:S(2)}) collective-permute-start(bf16[1536,512]{1,0:T(8,128)(2,1)S(1)} %copy.10), channel_id=1, source_target_pairs={{0,32},{32,64},{64,96},{96,128},{128,160},{160,192},{192,224},{224... | collective-permute-start | bytes 4718600 | tf_op jit(solution)/shard_map/while/body/eval_jaxpr/ppermute | solution.py:9
  267.7 127.4 %reduce-scatter.2.cloned.1.call-start = ((), (), s32[]{:S(2)}) async-start(), calls=%async_computation.1 | async-start | bytes 1081344 | tf_op jit(solution)/shard_map/while/body/eval_jaxpr/reduce_scatter | solution.py:35
  278.3 117.6 %collective-permute-start = (bf16[1536,512]{1,0:T(8,128)(2,1)S(1)}, bf16[1536,512]{1,0:T(8,128)(2,1)S(1)}, u32[]{:S(2)}, u32[]{:S(2)}) collective-permute-start(bf16[1536,512]{1,0:T(8,128)(2,1)S(1)} %copy.10), channel_id=1, source_target_pairs={{0,32},{32,64},{64,96},{96,128},{128,160},{160,192},{192,224},{224... | collective-permute-start | bytes 4718600 | tf_op jit(solution)/shard_map/while/body/eval_jaxpr/ppermute | solution.py:9
  395.9 127.5 %reduce-scatter.2.cloned.1.call-start = ((), (), s32[]{:S(2)}) async-start(), calls=%async_computation.1 | async-start | bytes 1081344 | tf_op jit(solution)/shard_map/while/body/eval_jaxpr/reduce_scatter | solution.py:35
  406.4 117.8 %collective-permute-start = (bf16[1536,512]{1,0:T(8,128)(2,1)S(1)}, bf16[1536,512]{1,0:T(8,128)(2,1)S(1)}, u32[]{:S(2)}, u32[]{:S(2)}) collective-permute-start(bf16[1536,512]{1,0:T(8,128)(2,1)S(1)} %copy.10), channel_id=1, source_target_pairs={{0,32},{32,64},{64,96},{96,128},{128,160},{160,192},{192,224},{224... | collective-permute-start | bytes 4718600 | tf_op jit(solution)/shard_map/while/body/eval_jaxpr/ppermute | solution.py:9
  524.2 127.7 %reduce-scatter.2.cloned.1.call-start = ((), (), s32[]{:S(2)}) async-start(), calls=%async_computation.1 | async-start | bytes 1081344 | tf_op jit(solution)/shard_map/while/body/eval_jaxpr/reduce_scatter | solution.py:35
  534.8 117.9 %collective-permute-start = (bf16[1536,512]{1,0:T(8,128)(2,1)S(1)}, bf16[1536,512]{1,0:T(8,128)(2,1)S(1)}, u32[]{:S(2)}, u32[]{:S(2)}) collective-permute-start(bf16[1536,512]{1,0:T(8,128)(2,1)S(1)} %copy.10), channel_id=1, source_target_pairs={{0,32},{32,64},{64,96},{96,128},{128,160},{160,192},{192,224},{224... | collective-permute-start | bytes 4718600 | tf_op jit(solution)/shard_map/while/body/eval_jaxpr/ppermute | solution.py:9
  652.6 127.7 %reduce-scatter.2.cloned.1.call-start = ((), (), s32[]{:S(2)}) async-start(), calls=%async_computation.1 | async-start | bytes 1081344 | tf_op jit(solution)/shard_map/while/body/eval_jaxpr/reduce_scatter | solution.py:35
  663.2 117.9 %collective-permute-start = (bf16[1536,512]{1,0:T(8,128)(2,1)S(1)}, bf16[1536,512]{1,0:T(8,128)(2,1)S(1)}, u32[]{:S(2)}, u32[]{:S(2)}) collective-permute-start(bf16[1536,512]{1,0:T(8,128)(2,1)S(1)} %copy.10), channel_id=1, source_target_pairs={{0,32},{32,64},{64,96},{96,128},{128,160},{160,192},{192,224},{224... | collective-permute-start | bytes 4718600 | tf_op jit(solution)/shard_map/while/body/eval_jaxpr/ppermute | solution.py:9
  781.1 127.7 %reduce-scatter.2.cloned.1.call-start = ((), (), s32[]{:S(2)}) async-start(), calls=%async_computation.1 | async-start | bytes 1081344 | tf_op jit(solution)/shard_map/while/body/eval_jaxpr/reduce_scatter | solution.py:35
  791.7 117.9 %collective-permute-start = (bf16[1536,512]{1,0:T(8,128)(2,1)S(1)}, bf16[1536,512]{1,0:T(8,128)(2,1)S(1)}, u32[]{:S(2)}, u32[]{:S(2)}) collective-permute-start(bf16[1536,512]{1,0:T(8,128)(2,1)S(1)} %copy.10), channel_id=1, source_target_pairs={{0,32},{32,64},{64,96},{96,128},{128,160},{160,192},{192,224},{224... | collective-permute-start | bytes 4718600 | tf_op jit(solution)/shard_map/while/body/eval_jaxpr/ppermute | solution.py:9
  909.6 127.7 %reduce-scatter.2.cloned.1.call-start = ((), (), s32[]{:S(2)}) async-start(), calls=%async_computation.1 | async-start | bytes 1081344 | tf_op jit(solution)/shard_map/while/body/eval_jaxpr/reduce_scatter | solution.py:35
  920.1 117.9 %collective-permute-start = (bf16[1536,512]{1,0:T(8,128)(2,1)S(1)}, bf16[1536,512]{1,0:T(8,128)(2,1)S(1)}, u32[]{:S(2)}, u32[]{:S(2)}) collective-permute-start(bf16[1536,512]{1,0:T(8,128)(2,1)S(1)} %copy.10), channel_id=1, source_target_pairs={{0,32},{32,64},{64,96},{96,128},{128,160},{160,192},{192,224},{224... | collective-permute-start | bytes 4718600 | tf_op jit(solution)/shard_map/while/body/eval_jaxpr/ppermute | solution.py:9
Sparse Core Ops, SparseCore 0:
  18.6 119.8 reduce-scatter.1
  149.9 116.9 reduce-scatter.1
  278.4 116.6 reduce-scatter.1
  406.6 116.8 reduce-scatter.1
  534.9 116.9 reduce-scatter.1
  663.3 116.9 reduce-scatter.1
  791.8 116.9 reduce-scatter.1
  920.2 116.9 reduce-scatter.1
where the time goes:
time: 1130 us
  waiting for transfers between devices  936 us (83%)
  blocking collectives  79.7 us (7%)
  matrix products  48.4 us (4%)
  loops' own time  24.6 us (2%)
  local copies, waits for them, and re-layouts  13.6 us (1%)
  between operations  13.4 us (1%)
    reduce_scatter x8, waiting for transfers between devices, turn(): reduced = lax.psum_scatter(part, 'group', scatter_dimension=0, tiled=True)  936 us
    psum x1, blocking collectives, on_device(): total = lax.psum(column, ('blk', 'group'))  79.7 us
    dot_general x24, matrix products, panel_product(): product = jnp.dot(block, piece, preferred_element_type=jnp.float32)  48.4 us
    another operation x1, loops' own time, on_device(): unused, expanded = lax.fori_loop(0, nblock, turn, (col_values, start_out))  24.6 us
  transfers between devices with their start and end apart: 16, of which 8 were waited for; matrix products, arithmetic and copies ran while one was open for 1% of the time, Pallas kernels for 0%

commit v1 on v0

--- a/solution.py
+++ b/solution.py
@@ -1,7 +1,17 @@
+import functools
 import jax
 import jax.numpy as jnp
 from jax import lax
 from jax.sharding import PartitionSpec as P
+
+
+def rounds_point(patch, peer_axis, mesh_ax):
+    for u in (peer_axis, mesh_ax):
+        patch = jax.lax.psum(patch, u)
+    return patch
+
+
+_derive_values = functools.partial(rounds_point, peer_axis="blk", mesh_ax="group")
 
 
 def shifted(shard, axis, by):
@@ -41,7 +51,7 @@
     unused, expanded = lax.fori_loop(0, nblock, turn, (col_values, start_out))
     squared = expanded * expanded
     column = jnp.sum(squared, axis=0)
-    total = lax.psum(column, ("blk", "group"))
+    total = _derive_values(column)
     scale = total / (nblock * rows_here) + 1e-06
     return squared / scale
 

time: 1130 us -> 1190 us (1.053)
  blocking collectives: 79.7 us -> 146 us
    psum x1 -> x2, blocking collectives: 79.7 us -> 146 us  [rounds_point(): patch = jax.lax.psum(patch, u)]
where the time goes in v1:
time: 1190 us
  waiting for transfers between devices  935 us (79%)
  blocking collectives  146 us (12%)
  matrix products  48 us (4%)
  loops' own time  25.2 us (2%)
  local copies, waits for them, and re-layouts  13.6 us (1%)
  between operations  13.4 us (1%)
    reduce_scatter x8, waiting for transfers between devices, turn(): reduced = lax.psum_scatter(part, 'group', scatter_dimension=0, tiled=True)  935 us
    psum x2, blocking collectives, rounds_point(): patch = jax.lax.psum(patch, u)  146 us
    dot_general x24, matrix products, panel_product(): product = jnp.dot(block, piece, preferred_element_type=jnp.float32)  48 us
    another operation x1, loops' own time, on_device(): unused, expanded = lax.fori_loop(0, nblock, turn, (col_values, start_out))  25.2 us
  transfers between devices with their start and end apart: 16, of which 8 were waited for; matrix products, arithmetic and copies ran while one was open for 1% of the time, Pallas kernels for 0%

profile of v1, /device:TPU:1, one launch (start us, length us, event | category | flops | bytes accessed | tf_op | source)
XLA Modules:
  0.0 1190.7 jit_solution(7623201862333923885)
XLA Ops:
  7.9 1029.5 %while.17 = (s32[]{:T(128)}, bf16[1536,512]{1,0:T(8,128)(2,1)S(1)}, f32[16,4096]{1,0:T(8,128)S(1)}, s32[]{:T(128)}, s32[1,8]{1,0:T(1,128)S(1)}, /*index=5*/s32[3...) while((s32[]{:T(128)}, bf16[1536,512]{1,0:T(8,128)(2,1)S(1)}, ...), condition=%wide.region_2.3_spmd, body=%wide.region_0.2_spmd.sunk | while | flops 806617088 | bytes 21137560 | solution.py:51
  12.4 2.0 convolution_select_fusion.5
  16.0 2.5 fusion.30
  18.5 2.2 collective-permute-start
  20.7 117.8 %reduce-scatter.2.cloned.1.call-done = f32[16,512]{1,0:T(8,128)} async-done(((f32[512,512]{1,0:T(8,128)}), f32[16,512]{1,0:T(8,128)}) %reduce-scatter.2.cloned.1.call-update) | async-done | bytes 32784 | tf_op jit(solution)/shard_map/while/body/eval_jaxpr/reduce_scatter | solution.py:45
  143.7 2.0 convolution_select_fusion.5
  147.3 2.5 fusion.30
  149.9 117.0 %reduce-scatter.2.cloned.1.call-done = f32[16,512]{1,0:T(8,128)} async-done(((f32[512,512]{1,0:T(8,128)}), f32[16,512]{1,0:T(8,128)}) %reduce-scatter.2.cloned.1.call-update) | async-done | bytes 32784 | tf_op jit(solution)/shard_map/while/body/eval_jaxpr/reduce_scatter | solution.py:45
  272.2 2.0 convolution_select_fusion.5
  275.7 2.5 fusion.30
  278.3 117.0 %reduce-scatter.2.cloned.1.call-done = f32[16,512]{1,0:T(8,128)} async-done(((f32[512,512]{1,0:T(8,128)}), f32[16,512]{1,0:T(8,128)}) %reduce-scatter.2.cloned.1.call-update) | async-done | bytes 32784 | tf_op jit(solution)/shard_map/while/body/eval_jaxpr/reduce_scatter | solution.py:45
  400.6 2.0 convolution_select_fusion.5
  402.6 1.5 convolution_select_fusion.6
  404.1 2.5 fusion.30
  406.7 116.7 %reduce-scatter.2.cloned.1.call-done = f32[16,512]{1,0:T(8,128)} async-done(((f32[512,512]{1,0:T(8,128)}), f32[16,512]{1,0:T(8,128)}) %reduce-scatter.2.cloned.1.call-update) | async-done | bytes 32784 | tf_op jit(solution)/shard_map/while/body/eval_jaxpr/reduce_scatter | solution.py:45
  528.7 2.0 convolution_select_fusion.5
  530.7 1.5 convolution_select_fusion.6
  532.2 2.5 fusion.30
  535.0 116.8 %reduce-scatter.2.cloned.1.call-done = f32[16,512]{1,0:T(8,128)} async-done(((f32[512,512]{1,0:T(8,128)}), f32[16,512]{1,0:T(8,128)}) %reduce-scatter.2.cloned.1.call-update) | async-done | bytes 32784 | tf_op jit(solution)/shard_map/while/body/eval_jaxpr/reduce_scatter | solution.py:45
  657.0 2.0 convolution_select_fusion.5
  659.1 1.5 convolution_select_fusion.6
  660.6 2.5 fusion.30
  663.3 117.0 %reduce-scatter.2.cloned.1.call-done = f32[16,512]{1,0:T(8,128)} async-done(((f32[512,512]{1,0:T(8,128)}), f32[16,512]{1,0:T(8,128)}) %reduce-scatter.2.cloned.1.call-update) | async-done | bytes 32784 | tf_op jit(solution)/shard_map/while/body/eval_jaxpr/reduce_scatter | solution.py:45
  785.6 2.0 convolution_select_fusion.5
  789.1 2.5 fusion.30
  792.0 116.5 %reduce-scatter.2.cloned.1.call-done = f32[16,512]{1,0:T(8,128)} async-done(((f32[512,512]{1,0:T(8,128)}), f32[16,512]{1,0:T(8,128)}) %reduce-scatter.2.cloned.1.call-update) | async-done | bytes 32784 | tf_op jit(solution)/shard_map/while/body/eval_jaxpr/reduce_scatter | solution.py:45
  913.8 2.0 convolution_select_fusion.5
  915.8 1.5 convolution_select_fusion.6
  917.3 2.5 fusion.30
  920.2 116.5 %reduce-scatter.2.cloned.1.call-done = f32[16,512]{1,0:T(8,128)} async-done(((f32[512,512]{1,0:T(8,128)}), f32[16,512]{1,0:T(8,128)}) %reduce-scatter.2.cloned.1.call-update) | async-done | bytes 32784 | tf_op jit(solution)/shard_map/while/body/eval_jaxpr/reduce_scatter | solution.py:45
  1037.5 34.3 %psum.14 = f32[4096]{0:T(1024)S(1)} all-reduce(f32[4096]{0:T(1024)S(1)} %multiply_reduce_fusion), channel_id=1, replica_groups=mesh['blk'=8,'group'=32] {'blk'}, use_global_device_ids=true, to_apply=%region_4.5 | all-reduce | flops 4096 | bytes 32768 | tf_op jit(solution)/shard_map/psum | solution.py:10
  1071.8 111.3 %psum.15 = f32[4096]{0:T(1024)S(1)} all-reduce(f32[4096]{0:T(1024)S(1)} %psum.14), channel_id=1, replica_groups=mesh['blk'=8,'group'=32] {'group'}, use_global_device_ids=true, to_apply=%region_5.6 | all-reduce | flops 4096 | bytes 32768 | tf_op jit(solution)/shard_map/psum | solution.py:10
  (85 shorter events, 27.0 us)
Async XLA Ops:
  6.5 1.4 copy-start
  6.5 1.4 copy-start.1
  6.5 1.4 copy-start.2
  7.9 130.5 %reduce-scatter.2.cloned.1.call-start = ((), (), s32[]{:S(2)}) async-start(), calls=%async_computation.1 | async-start | bytes 1081344 | tf_op jit(solution)/shard_map/while/body/eval_jaxpr/reduce_scatter | solution.py:45
  18.5 120.8 %collective-permute-start = (bf16[1536,512]{1,0:T(8,128)(2,1)S(1)}, bf16[1536,512]{1,0:T(8,128)(2,1)S(1)}, u32[]{:S(2)}, u32[]{:S(2)}) collective-permute-start(bf16[1536,512]{1,0:T(8,128)(2,1)S(1)} %copy.10), channel_id=1, source_target_pairs={{0,32},{32,64},{64,96},{96,128},{128,160},{160,192},{192,224},{224... | collective-permute-start | bytes 4718600 | tf_op jit(solution)/shard_map/while/body/eval_jaxpr/ppermute | solution.py:19
  139.2 127.7 %reduce-scatter.2.cloned.1.call-start = ((), (), s32[]{:S(2)}) async-start(), calls=%async_computation.1 | async-start | bytes 1081344 | tf_op jit(solution)/shard_map/while/body/eval_jaxpr/reduce_scatter | solution.py:45
  149.8 117.9 %collective-permute-start = (bf16[1536,512]{1,0:T(8,128)(2,1)S(1)}, bf16[1536,512]{1,0:T(8,128)(2,1)S(1)}, u32[]{:S(2)}, u32[]{:S(2)}) collective-permute-start(bf16[1536,512]{1,0:T(8,128)(2,1)S(1)} %copy.10), channel_id=1, source_target_pairs={{0,32},{32,64},{64,96},{96,128},{128,160},{160,192},{192,224},{224... | collective-permute-start | bytes 4718600 | tf_op jit(solution)/shard_map/while/body/eval_jaxpr/ppermute | solution.py:19
  267.7 127.7 %reduce-scatter.2.cloned.1.call-start = ((), (), s32[]{:S(2)}) async-start(), calls=%async_computation.1 | async-start | bytes 1081344 | tf_op jit(solution)/shard_map/while/body/eval_jaxpr/reduce_scatter | solution.py:45
  278.2 117.9 %collective-permute-start = (bf16[1536,512]{1,0:T(8,128)(2,1)S(1)}, bf16[1536,512]{1,0:T(8,128)(2,1)S(1)}, u32[]{:S(2)}, u32[]{:S(2)}) collective-permute-start(bf16[1536,512]{1,0:T(8,128)(2,1)S(1)} %copy.10), channel_id=1, source_target_pairs={{0,32},{32,64},{64,96},{96,128},{128,160},{160,192},{192,224},{224... | collective-permute-start | bytes 4718600 | tf_op jit(solution)/shard_map/while/body/eval_jaxpr/ppermute | solution.py:19
  396.1 127.3 %reduce-scatter.2.cloned.1.call-start = ((), (), s32[]{:S(2)}) async-start(), calls=%async_computation.1 | async-start | bytes 1081344 | tf_op jit(solution)/shard_map/while/body/eval_jaxpr/reduce_scatter | solution.py:45
  406.6 117.6 %collective-permute-start = (bf16[1536,512]{1,0:T(8,128)(2,1)S(1)}, bf16[1536,512]{1,0:T(8,128)(2,1)S(1)}, u32[]{:S(2)}, u32[]{:S(2)}) collective-permute-start(bf16[1536,512]{1,0:T(8,128)(2,1)S(1)} %copy.10), channel_id=1, source_target_pairs={{0,32},{32,64},{64,96},{96,128},{128,160},{160,192},{192,224},{224... | collective-permute-start | bytes 4718600 | tf_op jit(solution)/shard_map/while/body/eval_jaxpr/ppermute | solution.py:19
  524.2 127.6 %reduce-scatter.2.cloned.1.call-start = ((), (), s32[]{:S(2)}) async-start(), calls=%async_computation.1 | async-start | bytes 1081344 | tf_op jit(solution)/shard_map/while/body/eval_jaxpr/reduce_scatter | solution.py:45
  534.7 117.8 %collective-permute-start = (bf16[1536,512]{1,0:T(8,128)(2,1)S(1)}, bf16[1536,512]{1,0:T(8,128)(2,1)S(1)}, u32[]{:S(2)}, u32[]{:S(2)}) collective-permute-start(bf16[1536,512]{1,0:T(8,128)(2,1)S(1)} %copy.10), channel_id=1, source_target_pairs={{0,32},{32,64},{64,96},{96,128},{128,160},{160,192},{192,224},{224... | collective-permute-start | bytes 4718600 | tf_op jit(solution)/shard_map/while/body/eval_jaxpr/ppermute | solution.py:19
  652.5 127.7 %reduce-scatter.2.cloned.1.call-start = ((), (), s32[]{:S(2)}) async-start(), calls=%async_computation.1 | async-start | bytes 1081344 | tf_op jit(solution)/shard_map/while/body/eval_jaxpr/reduce_scatter | solution.py:45
  663.1 118.0 %collective-permute-start = (bf16[1536,512]{1,0:T(8,128)(2,1)S(1)}, bf16[1536,512]{1,0:T(8,128)(2,1)S(1)}, u32[]{:S(2)}, u32[]{:S(2)}) collective-permute-start(bf16[1536,512]{1,0:T(8,128)(2,1)S(1)} %copy.10), channel_id=1, source_target_pairs={{0,32},{32,64},{64,96},{96,128},{128,160},{160,192},{192,224},{224... | collective-permute-start | bytes 4718600 | tf_op jit(solution)/shard_map/while/body/eval_jaxpr/ppermute | solution.py:19
  781.1 127.5 %reduce-scatter.2.cloned.1.call-start = ((), (), s32[]{:S(2)}) async-start(), calls=%async_computation.1 | async-start | bytes 1081344 | tf_op jit(solution)/shard_map/while/body/eval_jaxpr/reduce_scatter | solution.py:45
  791.6 117.7 %collective-permute-start = (bf16[1536,512]{1,0:T(8,128)(2,1)S(1)}, bf16[1536,512]{1,0:T(8,128)(2,1)S(1)}, u32[]{:S(2)}, u32[]{:S(2)}) collective-permute-start(bf16[1536,512]{1,0:T(8,128)(2,1)S(1)} %copy.10), channel_id=1, source_target_pairs={{0,32},{32,64},{64,96},{96,128},{128,160},{160,192},{192,224},{224... | collective-permute-start | bytes 4718600 | tf_op jit(solution)/shard_map/while/body/eval_jaxpr/ppermute | solution.py:19
  909.3 127.4 %reduce-scatter.2.cloned.1.call-start = ((), (), s32[]{:S(2)}) async-start(), calls=%async_computation.1 | async-start | bytes 1081344 | tf_op jit(solution)/shard_map/while/body/eval_jaxpr/reduce_scatter | solution.py:45
  919.8 117.6 %collective-permute-start = (bf16[1536,512]{1,0:T(8,128)(2,1)S(1)}, bf16[1536,512]{1,0:T(8,128)(2,1)S(1)}, u32[]{:S(2)}, u32[]{:S(2)}) collective-permute-start(bf16[1536,512]{1,0:T(8,128)(2,1)S(1)} %copy.10), channel_id=1, source_target_pairs={{0,32},{32,64},{64,96},{96,128},{128,160},{160,192},{192,224},{224... | collective-permute-start | bytes 4718600 | tf_op jit(solution)/shard_map/while/body/eval_jaxpr/ppermute | solution.py:19
Sparse Core Ops, SparseCore 0:
  18.6 119.8 reduce-scatter.1
  149.9 116.9 reduce-scatter.1
  278.3 116.9 reduce-scatter.1
  406.7 116.6 reduce-scatter.1
  534.8 116.9 reduce-scatter.1
  663.2 117.0 reduce-scatter.1
  791.7 116.7 reduce-scatter.1
  919.9 116.6 reduce-scatter.1
